TPU v7x, 256 devices: a whole 4x4x8 slice. The times are simulated.
256 devices in a mesh: row: 16 (over z, core), col: 8 (over x, y_lo), vec: 2 (over y_hi).
Axes of the slice: x: 4, y: 4 (y_hi: 2, y_lo: 2; y = y_hi * 2 + y_lo), z: 8, core: 2. Of those that a mesh axis runs over, the one named last changes fastest.
Arguments:
- vectors: bfloat16 [16, 131072], P('vec', ('row', 'col')), may hold values from -6 to 6
- tile_vals: bfloat16 [16, 8, 256, 128, 128], P('row', 'col'), may hold values from -0.09375 to 0.09375
- tile_rows: int32 [16, 8, 256], P('row', 'col'), may hold values from 0 to 1023, as said below
- tile_cols: int32 [16, 8, 256], P('row', 'col'), may hold values from 0 to 1023, as said below
- tile_counts: int32 [16, 8], P('row', 'col'), may hold values from 1 to 256, as said below
Outputs:
- product: bfloat16 [16, 131072], P('vec', ('row', 'col'))
- gram: float32 [16, 16], P(None, 'vec')
Inputs may be any that keep to these rules, and one draw needn't show every extreme that they name: `tile_rows`: list [i, j] names tiles whose row index r has i * 64 <= r < (i + 1) * 64 and whose column index c has (c // 8) % (8) == j, that is the column's block of 8 tile rows, numbered c // 8, is held by column group j; live slots name distinct tiles with r >= c; slots at or beyond the count hold in-range indices that must be ignored. `tile_cols`: see tile_rows; the same slots. `tile_counts`: some lists are full in every draw; lists near the top of the triangle hold few tiles.
All inputs are finite; a program needn't handle non-finite values.
Results may differ from a plain program's by a relative error of at most 0.001.
Values may be sent and summed in bfloat16 or wider, within the bound.
A program may use at most 64 MiB of HBM per device.

v0:
```python
import math
import jax
import jax.numpy as jnp
from jax import lax
from jax.sharding import PartitionSpec as P


def shards(vectors, tile_vals, tile_rows, tile_cols, tile_counts):
    nrow = lax.axis_size("row")
    ncol = lax.axis_size("col")
    vlocal, width = vectors.shape
    tile = tile_vals.shape[-1]
    stretch = width // tile
    span = ncol * stretch
    colspan = nrow * stretch
    row_x = lax.all_gather(vectors, "col", axis=1, tiled=True)
    col_x = lax.all_gather(vectors, "row", axis=1, tiled=True)
    tiles = tile_vals[0, 0]
    rows = tile_rows[0, 0]
    cols = tile_cols[0, 0]
    count = tile_counts[0, 0]
    slots = jnp.arange(rows.shape[0], dtype=jnp.int32)
    live = slots < count
    mirror = live & (rows != cols)
    row_place = rows % span
    col_place = cols // span * stretch + cols % stretch
    row_blocks = row_x.reshape(vlocal, span, tile)
    col_blocks = col_x.reshape(vlocal, colspan, tile)
    picked_cols = jnp.take(col_blocks, col_place, axis=1)
    picked_rows = jnp.take(row_blocks, row_place, axis=1)
    down = jnp.einsum("tij,vtj->vti", tiles, picked_cols, preferred_element_type=jnp.float32)
    upper = jnp.einsum("tij,vti->vtj", tiles, picked_rows, preferred_element_type=jnp.float32)
    row_hit = (
        (row_place[None, :] == jnp.arange(span, dtype=jnp.int32)[:, None]) & live[None, :]
    ).astype(jnp.float32)
    col_hit = (
        (col_place[None, :] == jnp.arange(colspan, dtype=jnp.int32)[:, None]) & mirror[None, :]
    ).astype(jnp.float32)
    row_part = jnp.einsum("at,vti->vai", row_hit, down, precision=lax.Precision.HIGHEST).reshape(
        vlocal, span * tile
    )
    col_part = jnp.einsum("at,vti->vai", col_hit, upper, precision=lax.Precision.HIGHEST).reshape(
        vlocal, colspan * tile
    )
    row_whole = lax.psum(row_part, "col")
    col_whole = lax.psum(col_part, "row")
    row_share = lax.dynamic_slice_in_dim(row_whole, lax.axis_index("col") * width, width, 1)
    col_share = lax.dynamic_slice_in_dim(col_whole, lax.axis_index("row") * width, width, 1)
    image = row_share + col_share
    every_vector = lax.all_gather(vectors, "vec", axis=0, tiled=True)
    partial_gram = jnp.dot(
        every_vector.astype(jnp.float32), image.T, precision=lax.Precision.HIGHEST
    )
    gram = lax.psum(partial_gram, ("row", "col")) / math.sqrt(width * nrow * ncol)
    return (image.astype(jnp.bfloat16), gram)


def solution(mesh):
    return jax.shard_map(
        shards,
        mesh=mesh,
        in_specs=(
            P("vec", ("row", "col")),
            P("row", "col", None, None, None),
            P("row", "col", None),
            P("row", "col", None),
            P("row", "col"),
        ),
        out_specs=(P("vec", ("row", "col")), P(None, "vec")),
        check_vma=False,
    )
```

profile of v0, /device:TPU:8, one launch (start us, length us, event | category | flops | bytes accessed | tf_op | source)
XLA Modules:
  0.0 527.4 jit_solution(8425430569256399796)
XLA Ops:
  7.2 0.0 copy-start.1
  7.2 0.0 copy-start.2
  7.2 0.0 all-reduce.5.cloned.1.call-start
  7.2 28.5 %all_gather.10 = bf16[8,8192]{1,0:T(8,128)(2,1)S(1)} all-gather(bf16[8,1024]{1,0:T(8,128)(2,1)} %param.5), channel_id=1, replica_groups=mesh['row'=16,'col'=8,'vec'=2] {'col'}, dimensions={1}, use_global_device_ids=true | all-gather | bytes 147456 | tf_op jit(solution)/shard_map/all_gather | solution.py:16
  35.8 0.7 compare_select_fusion
  36.5 0.7 compare_and_fusion.1
  37.2 0.8 gather_fusion.1
  38.0 0.0 copy-start
  38.0 4.7 fusion
  42.7 0.4 copy.9
  43.8 0.0 copy-done.1
  43.8 0.0 copy-done.2
  43.8 0.6 convolution_bitcast_fusion
  44.5 0.2 copy.7
  44.7 1.1 copy.18
  45.8 0.0 all-reduce.5.cloned.1.call-update
  45.8 0.0 all-reduce.3.cloned.1.call-start
  45.9 0.0 copy-done
  45.9 20.7 %all_gather.9 = bf16[8,16384]{1,0:T(8,128)(2,1)S(1)} all-gather(bf16[8,1024]{1,0:T(8,128)(2,1)S(1)} %copy-done), channel_id=1, replica_groups=mesh['row'=16,'col'=8,'vec'=2] {'row'}, dimensions={1}, use_global_device_ids=true | all-gather | bytes 278528 | tf_op jit(solution)/shard_map/all_gather | solution.py:17
  66.6 0.8 gather_fusion
  67.4 6.8 %fusion.2 = f32[256,8,128]{2,1,0:T(8,128)S(1)} fusion(bf16[1,1,256,128,128]{4,3,2,1,0:T(8,128)(2,1)} %param.6, bf16[256,8,128]{2,1,0:T(8,128)(2,1)S(1)} %gather_fusion, pred[256]{0:T(512)(128)(4,1)S(1)} %get-tuple-element.2), kind=kOutput, calls=%fused_computation.4 | convolution fusion | flops 67371008 | bytes 9961728 | tf_op jit(solution)/shard_map/tij,vtj->vti/dot_general | solution.py:31
  74.2 0.6 convolution_bitcast_fusion.1
  74.8 0.9 copy.19
  75.7 0.0 all-reduce.3.cloned.1.call-update
  75.7 5.9 %all_gather.11 = bf16[16,1024]{1,0:T(8,128)(2,1)S(1)} all-gather(bf16[8,1024]{1,0:T(8,128)(2,1)S(1)} %copy-done), channel_id=1, replica_groups=mesh['row'=16,'col'=8,'vec'=2] {'vec'}, dimensions={0}, use_global_device_ids=true | all-gather | bytes 49152 | tf_op jit(solution)/shard_map/all_gather | solution.py:50
  81.7 77.3 %all-reduce.5.cloned.1.call-done = f32[8,16384]{1,0:T(8,128)} async-done(((f32[8,16384]{1,0:T(8,128)}), f32[8,16384]{1,0:T(8,128)}) %all-reduce.5.cloned.1.call-update) | async-done | bytes 524304 | tf_op jit(solution)/shard_map/psum | solution.py:46
  159.0 79.9 %all-reduce.3.cloned.1.call-done = f32[8,8192]{1,0:T(8,128)} async-done(((f32[8,8192]{1,0:T(8,128)}), f32[8,8192]{1,0:T(8,128)}) %all-reduce.3.cloned.1.call-update) | async-done | bytes 262160 | tf_op jit(solution)/shard_map/psum | solution.py:45
  238.9 0.9 convolution_bitcast_fusion.2
  239.8 278.8 %psum.23 = f32[16,8]{0,1:T(8,128)S(1)} all-reduce(f32[16,8]{0,1:T(8,128)S(1)} %convolution_bitcast_fusion.2), channel_id=1, replica_groups=mesh['row'=16,'col'=8,'vec'=2] {'row','col'}, use_global_device_ids=true, to_apply=%region_2.3 | all-reduce | flops 128 | bytes 1024 | tf_op jit(solution)/shard_map/psum | solution.py:54
  518.6 0.6 broadcast_multiply_fusion
  519.2 1.4 fusion.25
  (5 shorter events, 0.1 us)
Async XLA Ops:
  7.2 36.6 %copy-start.1 = (s32[1,1,256]{2,1,0:T(1,128)S(1)}, s32[1,1,256]{2,1,0:T(1,128)}, u32[]{:S(2)}) copy-start(s32[1,1,256]{2,1,0:T(1,128)} %param.7) | copy-start | bytes 3076
  7.2 36.6 %copy-start.2 = (s32[1,1,256]{2,1,0:T(1,128)S(1)}, s32[1,1,256]{2,1,0:T(1,128)}, u32[]{:S(2)}) copy-start(s32[1,1,256]{2,1,0:T(1,128)} %param.8) | copy-start | bytes 3076
  7.2 151.8 %all-reduce.5.cloned.1.call-start = ((), (), s32[]{:S(2)}) async-start(), calls=%async_computation.1 | async-start | bytes 1048576 | tf_op jit(solution)/shard_map/psum | solution.py:46
  38.0 7.9 %copy-start = (bf16[8,1024]{1,0:T(8,128)(2,1)S(1)}, bf16[8,1024]{1,0:T(8,128)(2,1)}, u32[]{:S(2)}) copy-start(bf16[8,1024]{1,0:T(8,128)(2,1)} %param.5) | copy-start | bytes 49156
  45.8 193.1 %all-reduce.3.cloned.1.call-start = ((), (), s32[]{:S(2)}) async-start(), calls=%async_computation | async-start | bytes 524288 | tf_op jit(solution)/shard_map/psum | solution.py:45
Sparse Core Ops, SparseCore 0:
  45.9 113.0 all-reduce.4
  161.6 77.2 all-reduce.2
where the time goes:
time: 528 us; the launch traced here: 527 us
  blocking collectives  334 us (63%)
  waiting for transfers between devices  157 us (30%)
  between operations  14.8 us (3%)
  matrix products  13.7 us (3%)
    psum x1, blocking collectives, shards(): lax.psum(partial_gram, ('row', 'col')) / math.sqrt(width * nrow * ncol)  279 us
    psum x1, waiting for transfers between devices, shards(): row_whole = lax.psum(row_part, 'col')  79.9 us
    psum x1, waiting for transfers between devices, shards(): col_whole = lax.psum(col_part, 'row')  77.3 us
    all_gather x1, blocking collectives, shards(): row_x = lax.all_gather(vectors, 'col', axis=1, tiled=True)  28.5 us
    all_gather x1, blocking collectives, shards(): col_x = lax.all_gather(vectors, 'row', axis=1, tiled=True)  20.7 us
  transfers between devices with their start and end apart: 2, of which 2 were waited for; matrix products, arithmetic and copies ran while one was open for 2% of the time, Pallas kernels for 0%

commit v1 on v0

--- a/solution.py
+++ b/solution.py
@@ -3,6 +3,10 @@
 import jax.numpy as jnp
 from jax import lax
 from jax.sharding import PartitionSpec as P
+
+
+def mark_blocks(work_x):
+    return jnp.sum(lax.all_gather(work_x, axis_name="col"), axis=0)
 
 
 def shards(vectors, tile_vals, tile_rows, tile_cols, tile_counts):
@@ -42,7 +46,7 @@
     col_part = jnp.einsum("at,vti->vai", col_hit, upper, precision=lax.Precision.HIGHEST).reshape(
         vlocal, colspan * tile
     )
-    row_whole = lax.psum(row_part, "col")
+    row_whole = mark_blocks(row_part)
     col_whole = lax.psum(col_part, "row")
     row_share = lax.dynamic_slice_in_dim(row_whole, lax.axis_index("col") * width, width, 1)
     col_share = lax.dynamic_slice_in_dim(col_whole, lax.axis_index("row") * width, width, 1)

time: 528 us -> 478 us (0.905)
  waiting for transfers between devices: 157 us -> 100 us
    psum x1 -> x0, waiting for transfers between devices: 79.9 us -> none  [shards(): row_whole = lax.psum(row_part, 'col')]
    psum x1, waiting for transfers between devices: 77.3 us -> 91 us  [shards(): col_whole = lax.psum(col_part, 'row')]
    all_gather x0 -> x1, waiting for transfers between devices: none -> 9.42 us  [mark_blocks(): return jnp.sum(lax.all_gather(work_x, axis_name='col'), axis=0)]
where the time goes in v1:
time: 478 us; the launch traced here: 473 us
  blocking collectives  334 us (70%)
  waiting for transfers between devices  100 us (21%)
  between operations  16.2 us (3%)
  matrix products  14.1 us (3%)
  other arithmetic  5.12 us (1%)
    psum x1, blocking collectives, shards(): lax.psum(partial_gram, ('row', 'col')) / math.sqrt(width * nrow * ncol)  277 us
    psum x1, waiting for transfers between devices, shards(): col_whole = lax.psum(col_part, 'row')  91 us
    all_gather x1, blocking collectives, shards(): row_x = lax.all_gather(vectors, 'col', axis=1, tiled=True)  29.2 us
    all_gather x1, blocking collectives, shards(): col_x = lax.all_gather(vectors, 'row', axis=1, tiled=True)  20.9 us
  transfers between devices with their start and end apart: 2, of which 2 were waited for; matrix products, arithmetic and copies ran while one was open for 2% of the time, Pallas kernels for 0%

profile of v1, /device:TPU:8, one launch (start us, length us, event | category | flops | bytes accessed | tf_op | source)
XLA Modules:
  0.0 473.5 jit_solution(6371742804245376323)
XLA Ops:
  8.0 0.0 copy-start
  8.0 0.0 copy-start.1
  8.0 0.0 all-gather.2.cloned.1.call-start
  8.7 20.9 %all_gather.12 = bf16[8,16384]{1,0:T(8,128)(2,1)S(1)} all-gather(bf16[8,1024]{1,0:T(8,128)(2,1)} %param.5), channel_id=1, replica_groups=mesh['row'=16,'col'=8,'vec'=2] {'row'}, dimensions={1}, use_global_device_ids=true | all-gather | bytes 278528 | tf_op jit(solution)/shard_map/all_gather | solution.py:21
  29.6 0.7 compare_select_fusion.1
  30.4 0.8 gather_fusion
  31.2 0.7 compare_and_fusion.1
  31.9 6.8 %fusion.4 = f32[8,256,128]{2,0,1:T(8,128)S(1)} fusion(bf16[1,1,256,128,128]{4,3,2,1,0:T(8,128)(2,1)} %param.6, bf16[256,8,128]{2,1,0:T(8,128)(2,1)S(1)} %gather_fusion, pred[256]{0:T(512)(128)(4,1)S(1)} %get-tuple-element.8), kind=kOutput, calls=%fused_computation.6 | convolution fusion | flops 67371008 | bytes 9961728 | tf_op jit(solution)/shard_map/tij,vtj->vti/dot_general | solution.py:35
  38.7 0.6 convolution_bitcast_fusion.1
  39.3 0.8 all_gather_reshape.3
  40.1 0.0 all-gather.2.cloned.1.call-update
  40.1 0.0 all-reduce.2.cloned.1.call-start
  40.2 0.0 copy-done
  40.2 29.2 %all_gather.14 = bf16[8,8192]{1,0:T(8,128)(2,1)S(1)} all-gather(bf16[8,1024]{1,0:T(8,128)(2,1)S(1)} %copy-done), channel_id=1, replica_groups=mesh['row'=16,'col'=8,'vec'=2] {'col'}, dimensions={1}, use_global_device_ids=true | all-gather | bytes 147456 | tf_op jit(solution)/shard_map/all_gather | solution.py:20
  69.4 0.0 copy-done.1
  69.4 0.8 gather_fusion.1
  70.2 4.8 %fusion.7 = f32[8,256,128]{2,0,1:T(8,128)S(1)} fusion(bf16[1,1,256,128,128]{4,3,2,1,0:T(8,128)(2,1)} %param.6, bf16[256,8,128]{2,1,0:T(8,128)(2,1)S(1)} %gather_fusion.1, pred[256]{0:T(512)(128)(4,1)S(1)} %get-tuple-element.4), kind=kOutput, calls=%fused_computation.7 | convolution fusion | flops 67371008 | bytes 9961728 | tf_op jit(solution)/shard_map/tij,vti->vtj/dot_general | solution.py:36
  75.0 1.0 convolution_bitcast_fusion
  76.0 0.2 copy.10
  76.2 1.1 copy.17
  77.3 0.0 all-reduce.2.cloned.1.call-update
  77.4 6.8 %all_gather.15 = bf16[16,1024]{1,0:T(8,128)(2,1)S(1)} all-gather(bf16[8,1024]{1,0:T(8,128)(2,1)S(1)} %copy-done), channel_id=1, replica_groups=mesh['row'=16,'col'=8,'vec'=2] {'vec'}, dimensions={0}, use_global_device_ids=true | all-gather | bytes 49152 | tf_op jit(solution)/shard_map/all_gather | solution.py:54
  84.2 9.4 %all-gather.2.cloned.1.call-done = f32[8,8,8192]{2,1,0:T(8,128)} async-done(((f32[1,8,8192]{2,1,0:T(8,128)}), f32[8,8,8192]{2,1,0:T(8,128)}) %all-gather.2.cloned.1.call-update) | async-done | bytes 2097168 | tf_op jit(solution)/shard_map/all_gather | solution.py:9
  93.6 1.7 reduce_sum.9
  95.3 91.0 %all-reduce.2.cloned.1.call-done = f32[8,16384]{1,0:T(8,128)} async-done(((f32[8,16384]{1,0:T(8,128)}), f32[8,16384]{1,0:T(8,128)}) %all-reduce.2.cloned.1.call-update) | async-done | bytes 524304 | tf_op jit(solution)/shard_map/psum | solution.py:50
  186.3 0.9 convolution_bitcast_fusion.2
  187.2 276.8 %psum.15 = f32[16,8]{0,1:T(8,128)S(1)} all-reduce(f32[16,8]{0,1:T(8,128)S(1)} %convolution_bitcast_fusion.2), channel_id=1, replica_groups=mesh['row'=16,'col'=8,'vec'=2] {'row','col'}, use_global_device_ids=true, to_apply=%region_2.3 | all-reduce | flops 128 | bytes 1024 | tf_op jit(solution)/shard_map/psum | solution.py:58
  464.0 0.6 broadcast_multiply_fusion
  464.6 1.4 fusion.30
  (4 shorter events, 0.0 us)
Async XLA Ops:
  8.0 32.2 %copy-start = (bf16[8,1024]{1,0:T(8,128)(2,1)S(1)}, bf16[8,1024]{1,0:T(8,128)(2,1)}, u32[]{:S(2)}) copy-start(bf16[8,1024]{1,0:T(8,128)(2,1)} %param.5) | copy-start | bytes 49156
  8.0 61.4 %copy-start.1 = (s32[1,1,256]{2,1,0:T(1,128)S(1)}, s32[1,1,256]{2,1,0:T(1,128)}, u32[]{:S(2)}) copy-start(s32[1,1,256]{2,1,0:T(1,128)} %param.7) | copy-start | bytes 3076
  8.0 85.6 %all-gather.2.cloned.1.call-start = ((), (), s32[]{:S(2)}) async-start(), calls=%async_computation | async-start | bytes 2359296 | tf_op jit(solution)/shard_map/all_gather | solution.py:9
  40.1 146.2 %all-reduce.2.cloned.1.call-start = ((), (), s32[]{:S(2)}) async-start(), calls=%async_computation.1 | async-start | bytes 1048576 | tf_op jit(solution)/shard_map/psum | solution.py:50
Sparse Core Ops, SparseCore 0:
  40.3 53.2 all-gather.1
Sparse Core Ops, SparseCore 1:
  77.5 108.8 all-reduce.1
